TPU v7x, 32 devices: a whole 2x2x4 slice. The times are simulated.
32 devices in a mesh: dp: 4 (over y, core), ctx: 2 (over x), tensor: 4 (over z).
Axes of the slice: x: 2, y: 2, z: 4, core: 2. Of those that a mesh axis runs over, the one named last changes fastest.
Arguments:
- layer_input: bfloat16 [4, 512, 8192], P('dp', ('ctx', 'tensor')), may hold values from -6 to 6
- queries: bfloat16 [4, 512, 8192], P('dp', 'ctx', 'tensor'), may hold values from -12 to 12
- forward_output: bfloat16 [4, 512, 8192], P('dp', 'ctx', 'tensor'), may hold values from -6 to 6
- attention_output_gradient: bfloat16 [4, 512, 8192], P('dp', 'ctx', 'tensor'), may hold values from -6 to 6
- key_weight: bfloat16 [8192, 1024], P(None, 'tensor'), may hold values from -3 to 3
- value_projection_weight: bfloat16 [8192, 1024], P(None, 'tensor'), may hold values from -0.0625 to 0.0625
- segment: int32 [4, 512], P('dp'), may hold values from 0 to 4, as said below
- block_table: int32 [4, 4, 4], P('dp'), may hold values from 0 to 1, as said below
- block_owner: int32 [4, 4], P('dp'), may hold values from 0 to 3, each once within a row
Outputs:
- query_grad: bfloat16 [4, 512, 8192], P('dp', 'ctx', 'tensor')
- input_grad: bfloat16 [4, 512, 8192], P('dp', ('ctx', 'tensor'))
- key_weight_grad: bfloat16 [8192, 1024], P(('dp', 'ctx'), 'tensor')
- value_weight_grad: bfloat16 [8192, 1024], P(('dp', 'ctx'), 'tensor')
Inputs may be any that keep to these rules, and one draw needn't show every extreme that they name: Along the logical positions of a group the segment never falls; the prompt (0) comes first and every rollout 1 to 4 is present. block_table[g, b, c] is 1 only where some position of logical block b may read some position of logical block c under the causal and segment rule; block_table[g, b, b] is 1 for every block; other such pairs may be 0. `block_owner`: each group's row holds every logical block once.
All inputs are finite; a program needn't handle non-finite values.
Results may differ from a plain program's by a relative error of at most 0.005.
The roundings to bfloat16 on the way count: a program that leaves them out, or rounds other values in their place, can miss the bound.
Values may be sent and summed in bfloat16 or wider, within the bound.
A program may use at most 128 MiB of HBM per device.

v0:
```python
import math
import jax
import jax.numpy as jnp
from jax import lax
from jax.sharding import PartitionSpec as P

HEAD_SIZE = 128
BLK = 128


def per_device(
    layer_input,
    queries,
    forward_output,
    attention_output_gradient,
    key_weight,
    value_projection_weight,
    segment,
    block_table,
    block_owner,
):
    softmax_scale = 1.0 / math.sqrt(HEAD_SIZE)
    local_rows = queries.shape[1]
    kv_local = key_weight.shape[1] // HEAD_SIZE
    q_local = queries.shape[2] // HEAD_SIZE
    queries_per_group = q_local // kv_local
    kv_width = kv_local * HEAD_SIZE
    gathered = lax.all_gather(layer_input, "tensor", axis=1, tiled=True)[0]
    projected_keys = jnp.dot(gathered, key_weight, preferred_element_type=jnp.float32)
    projected_values = jnp.dot(
        gathered, value_projection_weight, preferred_element_type=jnp.float32
    )
    kv_rows = jnp.concatenate([projected_keys, projected_values], axis=1).astype(jnp.bfloat16)
    owner_row = block_owner[0]
    segments_row = segment[0]
    table_row = block_table[0]
    blocks_here = local_rows // BLK
    ctx_index = lax.axis_index("ctx")
    own_blocks = lax.dynamic_slice_in_dim(owner_row, ctx_index * blocks_here, blocks_here)
    offsets = jnp.arange(BLK, dtype=jnp.int32)
    query_pos = (own_blocks[:, None] * BLK + offsets[None, :]).reshape(-1)
    query_seg = jnp.take(segments_row, query_pos)
    own_table = jnp.take(table_row, own_blocks, axis=0)
    query_heads = queries[0].reshape(local_rows, kv_local, queries_per_group, HEAD_SIZE)
    grad_heads = attention_output_gradient[0].reshape(
        local_rows, kv_local, queries_per_group, HEAD_SIZE
    )
    saved_heads = forward_output[0].reshape(local_rows, kv_local, queries_per_group, HEAD_SIZE)
    correction = jnp.sum(grad_heads.astype(jnp.float32) * saved_heads.astype(jnp.float32), axis=-1)
    correction = correction.transpose(1, 2, 0)

    def allowed_for(leading_row, row_count):
        key_blocks = lax.dynamic_slice_in_dim(owner_row, leading_row // BLK, row_count // BLK)
        key_pos = (key_blocks[:, None] * BLK + offsets[None, :]).reshape(-1)
        key_seg = jnp.take(segments_row, key_pos)
        table_part = jnp.take(own_table, key_blocks, axis=1) == 1
        table_full = jnp.broadcast_to(
            table_part[:, None, :, None], (blocks_here, BLK, row_count // BLK, BLK)
        )
        table_full = table_full.reshape(local_rows, row_count)
        same_tree = (key_seg[None, :] == 0) | (key_seg[None, :] == query_seg[:, None])
        return table_full & (key_pos[None, :] <= query_pos[:, None]) & same_tree

    def block_scores(block_rows, leading_row):
        row_count = block_rows.shape[0]
        block_keys = block_rows[:, :kv_width].reshape(row_count, kv_local, HEAD_SIZE)
        block_values = block_rows[:, kv_width:].reshape(row_count, kv_local, HEAD_SIZE)
        raw_scores = (
            jnp.einsum(
                "qhgd,khd->hgqk", query_heads, block_keys, preferred_element_type=jnp.float32
            )
            * softmax_scale
        )
        allowed = allowed_for(leading_row, row_count)
        return (jnp.where(allowed[None, None], raw_scores, -jnp.inf), block_keys, block_values)

    def stats_block(carried, block_rows, leading_row):
        running_max, running_sum = carried
        scores = block_scores(block_rows, leading_row)[0]
        new_max = jnp.maximum(running_max, jnp.max(scores, axis=-1))
        running_sum = running_sum * jnp.exp(running_max - new_max) + jnp.sum(
            jnp.exp(scores - new_max[..., None]), axis=-1
        )
        return (new_max, running_sum)

    def grads_block(carried, block_rows, leading_row, log_norm):
        query_sum, keyval_sum = carried
        row_count = block_rows.shape[0]
        scores, block_keys, block_values = block_scores(block_rows, leading_row)
        probabilities = jnp.exp(scores - log_norm[..., None])
        probs_low = probabilities.astype(jnp.bfloat16)
        value_gradient_rows = jnp.einsum(
            "hgqk,qhgd->khd", probs_low, grad_heads, preferred_element_type=jnp.float32
        )
        prob_grads = jnp.einsum(
            "qhgd,khd->hgqk", grad_heads, block_values, preferred_element_type=jnp.float32
        )
        score_low = (probabilities * (prob_grads - correction[..., None])).astype(jnp.bfloat16)
        query_sum = query_sum + jnp.einsum(
            "hgqk,khd->qhgd", score_low, block_keys, preferred_element_type=jnp.float32
        )
        key_gradient_rows = (
            jnp.einsum("hgqk,qhgd->khd", score_low, query_heads, preferred_element_type=jnp.float32)
            * softmax_scale
        )
        update = jnp.concatenate(
            [
                key_gradient_rows.reshape(row_count, kv_width),
                value_gradient_rows.reshape(row_count, kv_width),
            ],
            axis=1,
        )
        keyval_sum = lax.dynamic_update_slice_in_dim(keyval_sum, update, leading_row, 0)
        return (query_sum, keyval_sum)

    def over_blocks(block_step, carried, shard_part):
        row_count = shard_part.shape[0]
        block_size = math.gcd(row_count, max(512, local_rows))
        block_count = row_count // block_size
        pieces = shard_part.reshape(block_count, block_size, shard_part.shape[1])
        starts = block_size * jnp.arange(block_count, dtype=jnp.int32)

        def one_block(state_in, scan_item):
            block_rows, block_start = scan_item
            result = block_step(state_in, block_rows, block_start)
            return (result, None)

        carried, _ = lax.scan(one_block, carried, (pieces, starts))
        return carried

    stats_init = (
        jnp.full((kv_local, queries_per_group, local_rows), -1e30, jnp.float32),
        jnp.zeros((kv_local, queries_per_group, local_rows), jnp.float32),
    )
    seq_rows = local_rows * lax.axis_size("ctx")
    grads_init = (
        jnp.zeros((local_rows, kv_local, queries_per_group, HEAD_SIZE), jnp.float32),
        jnp.zeros((seq_rows, 2 * kv_width), jnp.float32),
    )
    running_max, running_sum = over_blocks(
        stats_block, stats_init, lax.all_gather(kv_rows, "ctx", axis=0, tiled=True)
    )
    log_norm = running_max + jnp.log(running_sum)

    def grads_fold(carried, shard_part):
        return over_blocks(
            lambda state, rows_in, start_in: grads_block(state, rows_in, start_in, log_norm),
            carried,
            shard_part,
        )

    query_sum, keyval_sum = grads_fold(
        grads_init, lax.all_gather(kv_rows, "ctx", axis=0, tiled=True)
    )
    own_grads = lax.psum_scatter(keyval_sum, "ctx", scatter_dimension=0, tiled=True).astype(
        jnp.bfloat16
    )
    query_grad = (
        (query_sum * softmax_scale).astype(jnp.bfloat16).reshape(1, local_rows, q_local * HEAD_SIZE)
    )
    term = lax.dot_general(
        own_grads[:, :kv_width],
        key_weight,
        (((1,), (1,)), ((), ())),
        preferred_element_type=jnp.float32,
    )
    input_grad = lax.psum_scatter(
        term
        + lax.dot_general(
            own_grads[:, kv_width:],
            value_projection_weight,
            (((1,), (1,)), ((), ())),
            preferred_element_type=jnp.float32,
        ),
        "tensor",
        scatter_dimension=0,
        tiled=True,
    )
    input_grad = input_grad.astype(jnp.bfloat16)[None]
    weight_sum = lax.psum_scatter(
        lax.dot_general(
            gathered, own_grads, (((0,), (0,)), ((), ())), preferred_element_type=jnp.float32
        ),
        ("dp", "ctx"),
        scatter_dimension=0,
        tiled=True,
    )
    key_weight_grad = weight_sum[:, :kv_width].astype(jnp.bfloat16)
    value_weight_grad = weight_sum[:, kv_width:].astype(jnp.bfloat16)
    return (query_grad, input_grad, key_weight_grad, value_weight_grad)


def solution(mesh):
    in_specs = (
        P("dp", ("ctx", "tensor"), None),
        P("dp", "ctx", "tensor"),
        P("dp", "ctx", "tensor"),
        P("dp", "ctx", "tensor"),
        P(None, "tensor"),
        P(None, "tensor"),
        P("dp", None),
        P("dp", None, None),
        P("dp", None),
    )
    out_specs = (
        P("dp", "ctx", "tensor"),
        P("dp", ("ctx", "tensor"), None),
        P(("dp", "ctx"), "tensor"),
        P(("dp", "ctx"), "tensor"),
    )
    return jax.shard_map(
        per_device, mesh=mesh, in_specs=in_specs, out_specs=out_specs, check_vma=False
    )
```

profile of v0, /device:TPU:0, one launch (start us, length us, event | category | flops | bytes accessed | tf_op | source)
XLA Modules:
  0.0 426.8 jit_solution(8074572103710751653)
XLA Ops:
  7.2 0.0 copy-start
  7.2 0.0 copy-start.10
  7.2 0.0 all-gather.2.cloned.1.call-start
  7.3 0.7 all-gather.2.cloned.1.call-update
  7.9 0.0 reduce-scatter.4.cloned.1.call-start
  8.0 0.7 bitcast_multiply_fusion.1
  8.7 0.1 compare_select_fusion.1
  8.7 3.5 gather_fusion.3
  12.3 0.8 bitcast_multiply_fusion
  13.1 0.1 fusion.26
  13.2 1.9 gather_fusion.1
  15.2 0.1 fusion.23
  15.2 0.6 gather_fusion
  15.8 0.1 compare_and_fusion.1
  15.9 0.1 broadcast_select_fusion
  16.0 0.1 copy.41
  16.1 0.6 gather_fusion.2
  16.6 0.1 bitcast_compare_fusion
  16.7 0.1 copy.42
  16.8 0.1 add_bitcast_fusion
  16.9 0.1 and_select_fusion.1
  17.0 0.1 broadcast_compare_fusion
  17.0 0.1 broadcast_in_dim.108
  17.2 0.2 fusion.19
  17.4 0.3 copy.43
  17.7 0.5 copy.69
  18.2 1.5 copy.71
  19.8 1.6 copy.53
  21.4 0.2 convert_bitcast_fusion
  21.6 0.4 copy.72
  22.0 0.9 multiply_reduce_fusion
  22.9 0.1 copy.48
  23.0 70.1 %all-gather.2.cloned.1.call-done = bf16[1,256,8192]{2,1,0:T(8,128)(2,1)} async-done(((bf16[1,64,8192]{2,1,0:T(8,128)(2,1)}), bf16[1,256,8192]{2,1,0:T(8,128)(2,1)}) %all-gather.2.cloned.1.call-update) | async-done | bytes 4194320 | tf_op jit(solution)/shard_map/all_gather | solution.py:28
  93.1 5.3 %fusion.16 = bf16[256,256]{0,1:T(8,128)(2,1)S(1)} fusion(bf16[8192,256]{1,0:T(8,128)(2,1)} %param.18, bf16[1,256,8192]{2,1,0:T(8,128)(2,1)} %all-gather.2.cloned.1.call-done), kind=kOutput, calls=%fused_computation.27 | convolution fusion | flops 1073807360 | bytes 8519680 | tf_op jit(solution)/shard_map/dot_general | solution.py:30
  98.5 0.6 copy-done.3
  99.0 1.9 fusion.13
  100.9 8.9 %all_gather.8 = bf16[512,512]{0,1:T(8,128)(2,1)S(1)} all-gather(bf16[256,512]{0,1:T(8,128)(2,1)S(1)} %pad_maximum_fusion.1), channel_id=1, replica_groups=mesh['dp'=4,'ctx'=2,'tensor'=4] {'ctx'}, dimensions={0}, use_global_device_ids=true | all-gather | bytes 786432 | tf_op jit(solution)/shard_map/all_gather | solution.py:153
  109.9 1.4 fusion.3
  111.3 0.0 copy-start.8
  111.3 1.7 exponential_reduce_fusion
  113.0 2.3 fusion.9
  115.4 2.9 fusion.1
  118.2 2.0 copy-done.5
  120.2 1.5 fusion.12
  121.7 1.0 pad_maximum_fusion
  122.7 0.0 reduce-scatter.4.cloned.1.call-update
  122.7 0.0 reduce-scatter.6.cloned.1.call-start
  122.8 19.1 %reduce-scatter.4.cloned.1.call-done = f32[256,512]{0,1:T(8,128)} async-done(((f32[512,512]{0,1:T(8,128)}), f32[256,512]{0,1:T(8,128)}) %reduce-scatter.4.cloned.1.call-update) | async-done | bytes 524304 | tf_op jit(solution)/shard_map/reduce_scatter | solution.py:155
  141.9 1.1 convert_element_type.47
  143.0 3.6 fusion.21
  146.6 4.5 %convolution_add_fusion = f32[256,8192]{1,0:T(8,128)} fusion(f32[256,8192]{1,0:T(8,128)S(1)} %fusion.21, bf16[8192,256]{1,0:T(8,128)(2,1)S(1)} %copy-done.4, bf16[256,512]{0,1:T(8,128)(2,1)S(1)} %convert_element_type.47), kind=kOutput, calls=%fused_computation.5 | convolution fusion | flops 1075838976 | bytes 21102592 | tf_op jit(solution)/shard_map/dot_general | solution.py:169
  151.2 0.0 reduce-scatter.6.cloned.1.call-update
  151.2 0.3 reduce-scatter.8.cloned.1.call-start
  151.5 10.9 %convolution_bitcast_fusion = f32[8192,512]{0,1:T(8,128)} fusion(bf16[256,512]{0,1:T(8,128)(2,1)S(1)} %convert_element_type.47, bf16[1,256,8192]{2,1,0:T(8,128)(2,1)} %all-gather.2.cloned.1.call-done), kind=kOutput, calls=%fused_computation.4 | convolution fusion | flops 2147483648 | bytes 21233664 | tf_op jit(solution)/shard_map/dot_general | solution.py:181
  162.4 0.0 reduce-scatter.8.cloned.1.call-update
  162.4 2.9 multiply_convert_fusion
  165.3 1.4 copy.54
  166.7 129.1 %reduce-scatter.6.cloned.1.call-done = f32[64,8192]{1,0:T(8,128)} async-done(((f32[256,8192]{1,0:T(8,128)}), f32[64,8192]{1,0:T(8,128)}) %reduce-scatter.6.cloned.1.call-update) | async-done | bytes 2097168 | tf_op jit(solution)/shard_map/reduce_scatter | solution.py:167
  295.8 2.7 convert_bitcast_fusion.1
  298.5 117.9 %reduce-scatter.8.cloned.1.call-done = f32[1024,512]{0,1:T(8,128)} async-done(((f32[8192,512]{0,1:T(8,128)}), f32[1024,512]{0,1:T(8,128)}) %reduce-scatter.8.cloned.1.call-update) | async-done | bytes 2097168 | tf_op jit(solution)/shard_map/reduce_scatter | solution.py:180
  416.4 1.7 convert.13
  418.1 0.1 fusion.27
  418.2 1.0 copy.56
  419.2 1.0 copy.55
  (27 shorter events, 0.2 us)
Async XLA Ops:
  7.2 1.6 copy-start
  7.2 8.0 %copy-start.10 = (s32[1,4]{1,0:T(1,128)S(1)}, s32[1,4]{1,0:T(1,128)}, u32[]{:S(2)}) copy-start(s32[1,4]{1,0:T(1,128)} %param.21) | copy-start | bytes 52
  7.2 8.1 %copy-start.9 = (s32[1,4,4]{2,1,0:T(4,128)S(1)}, s32[1,4,4]{2,1,0:T(4,128)}, u32[]{:S(2)}) copy-start(s32[1,4,4]{2,1,0:T(4,128)} %param.20) | copy-start | bytes 196
  7.2 10.5 %copy-start.7 = (bf16[1,256,2048]{2,1,0:T(8,128)(2,1)S(1)}, bf16[1,256,2048]{2,1,0:T(8,128)(2,1)}, u32[]{:S(2)}) copy-start(bf16[1,256,2048]{2,1,0:T(8,128)(2,1)} %param.14) | copy-start | bytes 3145732
  7.2 85.9 %all-gather.2.cloned.1.call-start = ((), (), s32[]{:S(2)}) async-start(), calls=%async_computation.3 | async-start | bytes 5242880 | tf_op jit(solution)/shard_map/all_gather | solution.py:28
  7.9 133.9 %reduce-scatter.4.cloned.1.call-start = ((), (), s32[]{:S(2)}) async-start(), calls=%async_computation.4 | async-start | bytes 1572864 | tf_op jit(solution)/shard_map/reduce_scatter | solution.py:155
  12.3 9.1 %copy-start.6 = (bf16[1,256,2048]{2,1,0:T(8,128)(2,1)S(1)}, bf16[1,256,2048]{2,1,0:T(8,128)(2,1)}, u32[]{:S(2)}) copy-start(bf16[1,256,2048]{2,1,0:T(8,128)(2,1)} %param.15) | copy-start | bytes 3145732
  93.1 5.3 %copy-start.2 = (bf16[1,256,8192]{2,1,0:T(8,128)(2,1)S(1)}, bf16[1,256,8192]{2,1,0:T(8,128)(2,1)}, u32[]{:S(2)}) copy-start(bf16[1,256,8192]{2,1,0:T(8,128)(2,1)} %all-gather.2.cloned.1.call-done) | copy-start | bytes 12582916
  93.1 5.9 %copy-start.3 = (bf16[8192,256]{1,0:T(8,128)(2,1)S(1)}, bf16[8192,256]{1,0:T(8,128)(2,1)}, u32[]{:S(2)}) copy-start(bf16[8192,256]{1,0:T(8,128)(2,1)} %param.17) | copy-start | bytes 12582916
  111.3 1.8 copy-start.8
  118.2 2.0 copy-start.5
  122.7 173.1 %reduce-scatter.6.cloned.1.call-start = ((), (), s32[]{:S(2)}) async-start(), calls=%async_computation.5 | async-start | bytes 10485760 | tf_op jit(solution)/shard_map/reduce_scatter | solution.py:167
  143.0 3.7 copy-start.4
  151.2 265.2 %reduce-scatter.8.cloned.1.call-start = ((), (), s32[]{:S(2)}) async-start(), calls=%async_computation.6 | async-start | bytes 18874368 | tf_op jit(solution)/shard_map/reduce_scatter | solution.py:180
  295.8 124.4 %copy-start.1 = (s32[1,512]{1,0:T(1,128)S(1)}, s32[1,512]{1,0:T(1,128)}, u32[]{:S(2)}) copy-start(s32[1,512]{1,0:T(1,128)} %param.19) | copy-start | bytes 6148
Sparse Core Ops, SparseCore 0:
  9.6 83.4 all-gather.1
  122.9 18.9 reduce-scatter.3
  151.3 144.4 reduce-scatter.5
  299.7 116.6 reduce-scatter.7
where the time goes:
time: 427 us
  waiting for transfers between devices  337 us (79%)
  matrix products  37.2 us (9%)
  local copies, waits for them, and re-layouts  17.4 us (4%)
  between operations  14.1 us (3%)
  other arithmetic  11.9 us (3%)
  blocking collectives  8.91 us (2%)
    reduce_scatter x1, waiting for transfers between devices, per_device(): lax.psum_scatter(term + lax.dot_general(own_grads[:, kv_width:], value_pr...  129 us
    reduce_scatter x1, waiting for transfers between devices, per_device(): lax.psum_scatter(lax.dot_general(gathered, own_grads, (((0,), (0,)), ((),...  118 us
    all_gather x1, waiting for transfers between devices, per_device(): gathered = lax.all_gather(layer_input, 'tensor', axis=1, tiled=True)[0]  70.1 us
    reduce_scatter x1, waiting for transfers between devices, per_device(): lax.psum_scatter(keyval_sum, 'ctx', scatter_dimension=0, tiled=True)  19.1 us
    dot_general x1, matrix products, per_device(): lax.dot_general(gathered, own_grads, (((0,), (0,)), ((), ())), preferred_...  10.9 us
    all_gather x1, blocking collectives, per_device(): lax.all_gather(kv_rows, 'ctx', axis=0, tiled=True)  8.91 us
  transfers between devices with their start and end apart: 4, of which 4 were waited for; matrix products, arithmetic and copies ran while one was open for 8% of the time, Pallas kernels for 0%

commit v1 on v0

--- a/solution.py
+++ b/solution.py
@@ -150,7 +150,10 @@
         )
 
     query_sum, keyval_sum = grads_fold(
-        grads_init, lax.all_gather(kv_rows, "ctx", axis=0, tiled=True)
+        grads_init,
+        jnp.concatenate(
+            lax.all_to_all(jnp.stack([kv_rows] * lax.axis_size("ctx")), "ctx", 0, 0), axis=0
+        ),
     )
     own_grads = lax.psum_scatter(keyval_sum, "ctx", scatter_dimension=0, tiled=True).astype(
         jnp.bfloat16

time: 427 us -> 435 us (1.019)
  transfers between devices with their start and end apart: 4 -> 5, of which waited for: 4 -> 5; matrix products, arithmetic and copies ran while one was open for 8% -> 8% of each run, Pallas kernels for 0% -> 0%
where the time goes in v1:
time: 435 us
  waiting for transfers between devices  340 us (78%)
  matrix products  38.5 us (9%)
  local copies, waits for them, and re-layouts  16.5 us (4%)
  between operations  14.1 us (3%)
  other arithmetic  12.7 us (3%)
  blocking collectives  8.79 us (2%)
    reduce_scatter x1, waiting for transfers between devices, per_device(): lax.psum_scatter(term + lax.dot_general(own_grads[:, kv_width:], value_pr...  129 us
    reduce_scatter x1, waiting for transfers between devices, per_device(): lax.psum_scatter(lax.dot_general(gathered, own_grads, (((0,), (0,)), ((),...  118 us
    all_gather x1, waiting for transfers between devices, per_device(): gathered = lax.all_gather(layer_input, 'tensor', axis=1, tiled=True)[0]  70.2 us
    reduce_scatter x1, waiting for transfers between devices, per_device(): lax.psum_scatter(keyval_sum, 'ctx', scatter_dimension=0, tiled=True)  18.3 us
    dot_general x1, matrix products, per_device(): lax.dot_general(gathered, own_grads, (((0,), (0,)), ((), ())), preferred_...  10.9 us
    all_gather x1, blocking collectives, per_device(): lax.all_gather(kv_rows, 'ctx', axis=0, tiled=True)  8.79 us
  transfers between devices with their start and end apart: 5, of which 5 were waited for; matrix products, arithmetic and copies ran while one was open for 8% of the time, Pallas kernels for 0%

profile of v1, /device:TPU:0, one launch (start us, length us, event | category | flops | bytes accessed | tf_op | source)
XLA Modules:
  0.0 434.8 jit_solution(18108098522488902661)
XLA Ops:
  7.3 0.7 all-gather.2.cloned.1.call-update
  8.0 0.7 bitcast_multiply_fusion.1
  8.6 0.1 compare_select_fusion.1
  8.7 3.5 gather_fusion.3
  12.2 0.8 bitcast_multiply_fusion
  13.1 0.1 fusion.28
  13.1 1.9 gather_fusion.1
  15.1 0.1 fusion.25
  15.2 0.6 gather_fusion
  15.8 0.1 compare_and_fusion.1
  15.8 0.1 broadcast_select_fusion
  15.9 0.1 copy.49
  16.0 0.6 gather_fusion.2
  16.6 0.1 bitcast_compare_fusion
  16.7 0.1 copy.50
  16.8 0.1 add_bitcast_fusion
  16.8 0.1 and_select_fusion.1
  16.9 0.1 broadcast_compare_fusion
  17.0 0.1 broadcast_in_dim.108
  17.1 0.2 fusion.21
  17.4 0.3 copy.51
  17.7 0.5 copy.83
  18.2 1.5 copy.85
  19.8 1.6 copy.64
  21.3 0.2 convert_bitcast_fusion
  21.6 0.4 copy.86
  22.0 0.9 multiply_reduce_fusion
  22.9 0.1 copy.59
  23.0 70.2 %all-gather.2.cloned.1.call-done = bf16[1,256,8192]{2,1,0:T(8,128)(2,1)} async-done(((bf16[1,64,8192]{2,1,0:T(8,128)(2,1)}), bf16[1,256,8192]{2,1,0:T(8,128)(2,1)}) %all-gather.2.cloned.1.call-update) | async-done | bytes 4194320 | tf_op jit(solution)/shard_map/all_gather | solution.py:28
  93.2 5.3 %fusion.18 = bf16[256,256]{0,1:T(8,128)(2,1)S(1)} fusion(bf16[8192,256]{1,0:T(8,128)(2,1)} %param.18, bf16[1,256,8192]{2,1,0:T(8,128)(2,1)} %all-gather.2.cloned.1.call-done), kind=kOutput, calls=%fused_computation.29 | convolution fusion | flops 1073807360 | bytes 8519680 | tf_op jit(solution)/shard_map/dot_general | solution.py:30
  98.5 0.6 copy-done.3
  99.1 1.9 fusion.15
  101.0 8.8 %all_gather.7 = bf16[512,512]{0,1:T(8,128)(2,1)S(1)} all-gather(bf16[256,512]{0,1:T(8,128)(2,1)S(1)} %pad_maximum_fusion.1), channel_id=1, replica_groups=mesh['dp'=4,'ctx'=2,'tensor'=4] {'ctx'}, dimensions={0}, use_global_device_ids=true | all-gather | bytes 786432 | tf_op jit(solution)/shard_map/all_gather | solution.py:141
  109.8 0.8 maximum_maximum_fusion
  110.6 3.5 all-to-all-start
  114.1 0.2 reduce-scatter.4.cloned.1.call-start
  114.3 1.4 fusion.4
  115.7 1.7 exponential_reduce_fusion
  117.5 4.1 all-to-all-done
  121.6 0.2 copy.47
  121.8 0.1 copy.56
  122.0 0.1 copy.48
  122.1 1.3 fusion.31
  123.4 2.3 fusion.11
  125.7 2.9 fusion.1
  128.6 1.5 fusion.14
  130.1 0.5 copy-done.5
  130.6 1.0 pad_maximum_fusion
  131.6 0.0 reduce-scatter.6.cloned.1.call-start
  131.7 18.3 %reduce-scatter.4.cloned.1.call-done = f32[256,512]{0,1:T(8,128)} async-done(((f32[512,512]{0,1:T(8,128)}), f32[256,512]{0,1:T(8,128)}) %reduce-scatter.4.cloned.1.call-update) | async-done | bytes 524304 | tf_op jit(solution)/shard_map/reduce_scatter | solution.py:158
  150.0 1.1 convert_element_type.54
  151.0 3.6 fusion.23
  154.7 4.5 %convolution_add_fusion = f32[256,8192]{1,0:T(8,128)} fusion(f32[256,8192]{1,0:T(8,128)S(1)} %fusion.23, bf16[8192,256]{1,0:T(8,128)(2,1)S(1)} %copy-done.4, bf16[256,512]{0,1:T(8,128)(2,1)S(1)} %convert_element_type.54), kind=kOutput, calls=%fused_computation.5 | convolution fusion | flops 1075838976 | bytes 21102592 | tf_op jit(solution)/shard_map/dot_general | solution.py:172
  159.3 0.3 reduce-scatter.8.cloned.1.call-start
  159.5 10.9 %convolution_bitcast_fusion = f32[8192,512]{0,1:T(8,128)} fusion(bf16[256,512]{0,1:T(8,128)(2,1)S(1)} %convert_element_type.54, bf16[1,256,8192]{2,1,0:T(8,128)(2,1)} %all-gather.2.cloned.1.call-done), kind=kOutput, calls=%fused_computation.4 | convolution fusion | flops 2147483648 | bytes 21233664 | tf_op jit(solution)/shard_map/dot_general | solution.py:184
  170.5 2.9 multiply_convert_fusion
  173.4 1.4 copy.65
  174.8 129.1 %reduce-scatter.6.cloned.1.call-done = f32[64,8192]{1,0:T(8,128)} async-done(((f32[256,8192]{1,0:T(8,128)}), f32[64,8192]{1,0:T(8,128)}) %reduce-scatter.6.cloned.1.call-update) | async-done | bytes 2097168 | tf_op jit(solution)/shard_map/reduce_scatter | solution.py:170
  303.9 2.7 convert_bitcast_fusion.1
  306.6 117.9 %reduce-scatter.8.cloned.1.call-done = f32[1024,512]{0,1:T(8,128)} async-done(((f32[8192,512]{0,1:T(8,128)}), f32[1024,512]{0,1:T(8,128)}) %reduce-scatter.8.cloned.1.call-update) | async-done | bytes 2097168 | tf_op jit(solution)/shard_map/reduce_scatter | solution.py:183
  424.5 1.7 convert.17
  426.2 0.1 fusion.29
  426.3 1.0 copy.67
  427.3 1.0 copy.66
  (35 shorter events, 0.3 us)
Async XLA Ops:
  7.2 1.5 copy-start
  7.2 7.9 %copy-start.10 = (s32[1,4]{1,0:T(1,128)S(1)}, s32[1,4]{1,0:T(1,128)}, u32[]{:S(2)}) copy-start(s32[1,4]{1,0:T(1,128)} %param.21) | copy-start | bytes 52
  7.2 8.0 %copy-start.9 = (s32[1,4,4]{2,1,0:T(4,128)S(1)}, s32[1,4,4]{2,1,0:T(4,128)}, u32[]{:S(2)}) copy-start(s32[1,4,4]{2,1,0:T(4,128)} %param.20) | copy-start | bytes 196
  7.2 10.5 %copy-start.7 = (bf16[1,256,2048]{2,1,0:T(8,128)(2,1)S(1)}, bf16[1,256,2048]{2,1,0:T(8,128)(2,1)}, u32[]{:S(2)}) copy-start(bf16[1,256,2048]{2,1,0:T(8,128)(2,1)} %param.14) | copy-start | bytes 3145732
  7.2 86.0 %all-gather.2.cloned.1.call-start = ((), (), s32[]{:S(2)}) async-start(), calls=%async_computation.4 | async-start | bytes 5242880 | tf_op jit(solution)/shard_map/all_gather | solution.py:28
  12.2 9.1 %copy-start.6 = (bf16[1,256,2048]{2,1,0:T(8,128)(2,1)S(1)}, bf16[1,256,2048]{2,1,0:T(8,128)(2,1)}, u32[]{:S(2)}) copy-start(bf16[1,256,2048]{2,1,0:T(8,128)(2,1)} %param.15) | copy-start | bytes 3145732
  93.2 5.3 %copy-start.2 = (bf16[1,256,8192]{2,1,0:T(8,128)(2,1)S(1)}, bf16[1,256,8192]{2,1,0:T(8,128)(2,1)}, u32[]{:S(2)}) copy-start(bf16[1,256,8192]{2,1,0:T(8,128)(2,1)} %all-gather.2.cloned.1.call-done) | copy-start | bytes 12582916
  93.2 5.9 %copy-start.3 = (bf16[8192,256]{1,0:T(8,128)(2,1)S(1)}, bf16[8192,256]{1,0:T(8,128)(2,1)}, u32[]{:S(2)}) copy-start(bf16[8192,256]{1,0:T(8,128)(2,1)} %param.17) | copy-start | bytes 12582916
  110.6 10.9 %all-to-all-start = ((bf16[2,256,512]{1,2,0:T(8,128)(2,1)}), bf16[2,256,512]{1,2,0:T(8,128)(2,1)S(1)}, u32[]{:S(2)}, u32[]{:S(2)}) async-start(bf16[2,256,512]{1,2,0:T(8,128)(2,1)} %maximum_maximum_fusion), calls=%async_computation | async-start | bytes 1048576 | tf_op jit(solution)/shard_map/all_to_all | solution.py:155
  114.1 35.8 %reduce-scatter.4.cloned.1.call-start = ((), (), s32[]{:S(2)}) async-start(), calls=%async_computation.5 | async-start | bytes 1572864 | tf_op jit(solution)/shard_map/reduce_scatter | solution.py:158
  122.1 1.3 copy-start.8
  128.6 2.0 copy-start.5
  131.6 172.3 %reduce-scatter.6.cloned.1.call-start = ((), (), s32[]{:S(2)}) async-start(), calls=%async_computation.6 | async-start | bytes 10485760 | tf_op jit(solution)/shard_map/reduce_scatter | solution.py:170
  151.0 3.7 copy-start.4
  159.3 265.2 %reduce-scatter.8.cloned.1.call-start = ((), (), s32[]{:S(2)}) async-start(), calls=%async_computation.7 | async-start | bytes 18874368 | tf_op jit(solution)/shard_map/reduce_scatter | solution.py:183
  303.9 124.4 %copy-start.1 = (s32[1,512]{1,0:T(1,128)S(1)}, s32[1,512]{1,0:T(1,128)}, u32[]{:S(2)}) copy-start(s32[1,512]{1,0:T(1,128)} %param.19) | copy-start | bytes 6148
Sparse Core Ops, SparseCore 0:
  9.6 83.5 all-gather.1
  131.8 18.1 reduce-scatter.3
  159.4 144.4 reduce-scatter.5
  307.7 116.6 reduce-scatter.7
